TPU v7x, 32 devices: a whole 2x2x4 slice. The times are simulated.
32 devices in a mesh: rep: 2 (over y), ep: 16 (over z, x, core).
Axes of the slice: x: 2, y: 2, z: 4, core: 2. Of those that a mesh axis runs over, the one named last changes fastest.
Arguments:
- tokens: bfloat16 [512, 2048], P(('rep', 'ep')), may hold values from -6 to 6
- logits: float32 [512, 8], P(('rep', 'ep')), may hold values from -6 to 6
- expert_ids: int32 [512, 8], P(('rep', 'ep')), may hold values from 0 to 15, all different within a row; in each aligned block of 16 rows (0 to 15, 16 to 31, ...) at most 16 rows name the same one
- w_gate_up: bfloat16 [16, 2, 2048, 1536], P('ep', None, None, 'rep'), may hold values from -0.125 to 0.125
- w_down: bfloat16 [16, 1536, 2048], P('ep', None, 'rep'), may hold values from -0.15625 to 0.15625
Outputs:
- mixed: bfloat16 [512, 2048], P(('rep', 'ep'))
Inputs may be any that keep to these rules, and one draw needn't show every extreme that they name: `expert_ids`: each token names 8 different experts; the 16 tokens of one device name any one expert at most 16 times.
All inputs are finite; a program needn't handle non-finite values.
Results may differ from a plain program's by a relative error of at most 0.0057.
Values may be sent and summed in bfloat16 or wider, within the bound.
A program may use at most 64 MiB of HBM per device.

v0:
```python
import jax
import jax.numpy as jnp
from jax import lax
from jax.sharding import PartitionSpec as P


def slot_plan(choice_ids, expert_count, capacity):
    queue_len, picks = choice_ids.shape
    flat_ids = choice_ids.reshape(queue_len * picks)
    position = jnp.arange(queue_len * picks, dtype=jnp.int32)
    earlier = (flat_ids[:, None] == flat_ids[None, :]) & (position[None, :] < position[:, None])
    slot_rank = jnp.sum(earlier.astype(jnp.int32), axis=1)
    target = flat_ids * capacity + slot_rank
    columns = jnp.arange(expert_count * capacity, dtype=jnp.int32)
    onehot = target[:, None] == columns[None, :]
    return onehot.reshape(queue_len, picks, expert_count * capacity)


def dispatch_rows(onehot, tokens):
    placing = jnp.sum(onehot.astype(jnp.bfloat16), axis=1)
    return jnp.dot(placing.T, tokens, preferred_element_type=jnp.float32).astype(jnp.bfloat16)


def to_owners(outgoing):
    return lax.all_to_all(outgoing, "ep", split_axis=0, concat_axis=0, tiled=True)


def to_sources(results):
    return lax.all_to_all(results, "ep", split_axis=0, concat_axis=0, tiled=True)


def full_units(quarter):
    return lax.all_gather(quarter, "rep", axis=1, tiled=True)


def body(tokens, logits, expert_ids, w_gate_up, w_down):
    expert_count = lax.axis_size("ep")
    queue_len, picks = expert_ids.shape
    features = tokens.shape[1]
    capacity = max(2, min(queue_len, 2 * queue_len * picks // expert_count))
    slot_total = expert_count * capacity
    onehot = slot_plan(expert_ids, expert_count, capacity)
    scaled = jnp.exp(logits)
    weights = scaled / jnp.sum(scaled, axis=1, keepdims=True)
    combine = jnp.sum(weights[:, :, None] * onehot.astype(jnp.float32), axis=1)
    gate_weight = w_gate_up[0, 0]
    up_weight = w_gate_up[0, 1]
    down_weight = w_down[0]
    received = to_owners(dispatch_rows(onehot, tokens).reshape(expert_count, capacity, features))
    slot_rows = received.reshape(slot_total, features)
    portion = lax.all_gather(slot_rows, "rep", axis=0, tiled=True)
    gate_part = jnp.dot(portion, gate_weight, preferred_element_type=jnp.float32)
    upper = jnp.dot(portion, up_weight, preferred_element_type=jnp.float32)
    quarter = (jax.nn.silu(gate_part) * upper).astype(jnp.bfloat16)
    hidden = full_units(quarter)
    partial_out = jnp.dot(hidden, down_weight, preferred_element_type=jnp.float32).astype(
        jnp.bfloat16
    )
    own_rows = lax.all_to_all(partial_out, "rep", split_axis=0, concat_axis=1, tiled=True)
    returned = to_sources(own_rows.reshape(expert_count, capacity, features))
    values = returned.reshape(slot_total, features)
    mixed = jnp.dot(combine, values.astype(jnp.float32), precision=lax.Precision.HIGHEST)
    return mixed.astype(jnp.bfloat16)


def solution(mesh):
    in_specs = (
        P(("rep", "ep"), None),
        P(("rep", "ep"), None),
        P(("rep", "ep"), None),
        P("ep", None, None, "rep"),
        P("ep", None, "rep"),
    )
    out_specs = P(("rep", "ep"), None)
    return jax.shard_map(body, mesh=mesh, in_specs=in_specs, out_specs=out_specs, check_vma=False)
```

profile of v0, /device:TPU:0, one launch (start us, length us, event | category | flops | bytes accessed | tf_op | source)
XLA Modules:
  0.0 173.4 jit_solution(292772381987471089)
XLA Ops:
  6.5 0.0 copy-start
  6.5 0.0 all-gather.3.cloned.1.call-start
  6.5 0.9 copy.17
  7.4 0.1 eq.29
  7.5 0.2 convert_reduce_fusion
  7.7 0.1 reduce_sum.42
  7.8 0.1 fusion.14
  8.0 1.3 convolution_convert_fusion
  9.3 32.0 %all_to_all.26 = bf16[16,16,2048]{2,1,0:T(8,128)(2,1)} all-to-all(bf16[16,16,2048]{2,1,0:T(8,128)(2,1)S(1)} %bitcast.26), channel_id=1, replica_groups=mesh['rep'=2,'ep'=16] {'ep'}, dimensions={0} | all-to-all | bytes 2097152 | tf_op jit(solution)/shard_map/all_to_all | solution.py:25
  41.2 0.0 all-gather.3.cloned.1.call-update
  41.3 0.0 all-gather.5.cloned.1.call-start
  41.3 33.6 %all-gather.3.cloned.1.call-done = bf16[512,2048]{1,0:T(8,128)(2,1)} async-done(((bf16[256,2048]{1,0:T(8,128)(2,1)}), bf16[512,2048]{1,0:T(8,128)(2,1)}) %all-gather.3.cloned.1.call-update) | async-done | bytes 2097168 | tf_op jit(solution)/shard_map/all_gather | solution.py:51
  74.9 0.0 copy-start.2
  74.9 4.5 %fusion.4 = f32[512,768]{1,0:T(8,128)S(1)} fusion(bf16[512,2048]{1,0:T(8,128)(2,1)} %all-gather.3.cloned.1.call-done, bf16[1,2,2048,768]{3,2,1,0:T(8,128)(2,1)} %param.8), kind=kOutput, calls=%fused_computation.4 | convolution fusion | flops 1610612736 | bytes 6815744 | tf_op jit(solution)/shard_map/dot_general | solution.py:52
  79.4 0.0 copy-done.2
  79.4 4.7 %multiply_convert_fusion = bf16[512,768]{1,0:T(8,128)(2,1)} fusion(f32[512,768]{1,0:T(8,128)S(1)} %fusion.4, bf16[512,2048]{1,0:T(8,128)(2,1)S(1)} %copy-done.2, bf16[1,2,2048,768]{3,2,1,0:T(8,128)(2,1)} %param.8), kind=kOutput, calls=%fused_computation.10 | convolution fusion | flops 1612972032 | bytes 7602176 | tf_op jit(solution)/shard_map/dot_general | solution.py:53
  84.1 0.0 all-gather.5.cloned.1.call-update
  84.1 27.3 %all-gather.5.cloned.1.call-done = bf16[512,1536]{1,0:T(8,128)(2,1)} async-done(((bf16[512,768]{1,0:T(8,128)(2,1)}), bf16[512,1536]{1,0:T(8,128)(2,1)}) %all-gather.5.cloned.1.call-update) | async-done | bytes 1572880 | tf_op jit(solution)/shard_map/all_gather | solution.py:33
  111.4 0.0 copy-done
  111.4 3.2 %fusion.10 = bf16[512,1024]{1,0:T(8,128)(2,1)S(1)} fusion(bf16[512,1536]{1,0:T(8,128)(2,1)} %all-gather.5.cloned.1.call-done, bf16[1,1536,1024]{2,1,0:T(8,128)(2,1)S(1)} %copy-done), kind=kOutput, calls=%fused_computation.11 | convolution fusion | flops 1611137024 | bytes 5767168 | tf_op jit(solution)/shard_map/dot_general | solution.py:56
  114.6 16.2 %all_to_all.27 = bf16[2,256,1024]{2,1,0:T(8,128)(2,1)S(1)} all-to-all(bf16[2,256,1024]{2,1,0:T(8,128)(2,1)S(1)} %bitcast.28), channel_id=1, replica_groups=mesh['rep'=2,'ep'=16] {'rep'}, dimensions={0} | all-to-all | bytes 2097152 | tf_op jit(solution)/shard_map/all_to_all | solution.py:59
  130.8 2.1 %copy.20 = bf16[256,2,1024]{2,1,0:T(2,128)(2,1)} copy(bf16[256,2,1024]{2,0,1:T(8,128)(2,1)S(1)} %bitcast.27) | data formatting | bytes 2097152 | tf_op jit(solution)/shard_map/all_to_all | solution.py:59
  132.9 0.0 copy-start.1
  132.9 2.6 %reshape.40 = bf16[16,16,2048]{2,1,0:T(8,128)(2,1)} reshape(bf16[256,2,1024]{2,1,0:T(2,128)(2,1)} %copy.20) | data formatting | bytes 2097152 | tf_op jit(solution)/shard_map/reshape | solution.py:60
  135.5 5.7 %all-to-all-start.2 = ((bf16[16,16,2048]{2,1,0:T(8,128)(2,1)}), bf16[16,16,2048]{2,1,0:T(8,128)(2,1)}, u32[]{:S(2)}, u32[]{:S(2)}) async-start(bf16[16,16,2048]{2,1,0:T(8,128)(2,1)} %reshape.40), calls=%async_computation.2 | async-start | bytes 2097152 | tf_op jit(solution)/shard_map/all_to_all | solution.py:29
  141.2 0.0 copy-done.1
  141.3 0.1 copy.19
  141.3 0.1 select_reduce_fusion
  141.5 22.7 %all-to-all-done.2 = bf16[16,16,2048]{2,1,0:T(8,128)(2,1)} async-done(((bf16[16,16,2048]{2,1,0:T(8,128)(2,1)}), bf16[16,16,2048]{2,1,0:T(8,128)(2,1)}, u32[]{:S(2)}, u32[]{:S(2)}) %all-to-all-start.2) | async-done | bytes 1048608 | tf_op jit(solution)/shard_map/all_to_all | solution.py:29
  164.2 2.4 %convolution_convert_fusion.1 = bf16[16,2048]{1,0:T(8,128)(2,1)} fusion(f32[16,256]{1,0:T(8,128)S(1)} %select_reduce_fusion, bf16[256,2048]{1,0:T(8,128)(2,1)} %bitcast.7), kind=kOutput, calls=%fused_computation.9 | convolution fusion | flops 100696064 | bytes 1130496 | tf_op jit(solution)/shard_map/dot_general | solution.py:62
  (3 shorter events, 0.0 us)
Async XLA Ops:
  6.5 104.9 %copy-start = (bf16[1,1536,1024]{2,1,0:T(8,128)(2,1)S(1)}, bf16[1,1536,1024]{2,1,0:T(8,128)(2,1)}, u32[]{:S(2)}) copy-start(bf16[1,1536,1024]{2,1,0:T(8,128)(2,1)} %param.9) | copy-start | bytes 9437188
  6.5 68.4 %all-gather.3.cloned.1.call-start = ((), (), s32[]{:S(2)}) async-start(), calls=%async_computation.3 | async-start | bytes 3145728 | tf_op jit(solution)/shard_map/all_gather | solution.py:51
  41.3 70.2 %all-gather.5.cloned.1.call-start = ((), (), s32[]{:S(2)}) async-start(), calls=%async_computation.4 | async-start | bytes 2359296 | tf_op jit(solution)/shard_map/all_gather | solution.py:33
  74.9 4.5 %copy-start.2 = (bf16[512,2048]{1,0:T(8,128)(2,1)S(1)}, bf16[512,2048]{1,0:T(8,128)(2,1)}, u32[]{:S(2)}) copy-start(bf16[512,2048]{1,0:T(8,128)(2,1)} %all-gather.3.cloned.1.call-done) | copy-start | bytes 6291460
  132.9 8.3 %copy-start.1 = (f32[16,8]{0,1:T(8,128)S(1)}, f32[16,8]{0,1:T(8,128)}, u32[]{:S(2)}) copy-start(f32[16,8]{0,1:T(8,128)} %param.6) | copy-start | bytes 1540
  135.5 28.6 %all-to-all-start.2 = ((bf16[16,16,2048]{2,1,0:T(8,128)(2,1)}), bf16[16,16,2048]{2,1,0:T(8,128)(2,1)}, u32[]{:S(2)}, u32[]{:S(2)}) async-start(bf16[16,16,2048]{2,1,0:T(8,128)(2,1)} %reshape.40), calls=%async_computation.2 | async-start | bytes 2097152 | tf_op jit(solution)/shard_map/all_to_all | solution.py:29
Sparse Core Ops, SparseCore 0:
  41.4 33.4 all-gather.2
  84.2 27.1 all-gather.4
where the time goes:
time: 175 us; the launch traced here: 173 us
  waiting for transfers between devices  83.7 us (48%)
  blocking collectives  48.1 us (27%)
  matrix products  16 us (9%)
  between operations  13.5 us (8%)
  local copies, waits for them, and re-layouts  5.91 us (3%)
  starting transfers between devices  5.71 us (3%)
    all_gather x1, waiting for transfers between devices, body(): portion = lax.all_gather(slot_rows, 'rep', axis=0, tiled=True)  33.6 us
    all_to_all x1, blocking collectives, to_owners(): lax.all_to_all(outgoing, 'ep', split_axis=0, concat_axis=0, tiled=True)  32 us
    all_gather x1, waiting for transfers between devices, full_units(): return lax.all_gather(quarter, 'rep', axis=1, tiled=True)  27.3 us
    all_to_all x1, waiting for transfers between devices, to_sources(): lax.all_to_all(results, 'ep', split_axis=0, concat_axis=0, tiled=True)  22.7 us
    all_to_all x1, blocking collectives, body(): lax.all_to_all(partial_out, 'rep', split_axis=0, concat_axis=1, tiled=True)  16.2 us
    all_to_all x1, starting transfers between devices, to_sources(): lax.all_to_all(results, 'ep', split_axis=0, concat_axis=0, tiled=True)  5.67 us
    dot_general x1, matrix products, body(): upper = jnp.dot(portion, up_weight, preferred_element_type=jnp.float32)  4.68 us
    dot_general x1, matrix products, body(): jnp.dot(portion, gate_weight, preferred_element_type=jnp.float32)  4.45 us
  transfers between devices with their start and end apart: 3, of which 3 were waited for; matrix products, arithmetic and copies ran while one was open for 0% of the time, Pallas kernels for 0%

commit v1 on v0

--- a/solution.py
+++ b/solution.py
@@ -1,6 +1,10 @@
+import functools
+
 import jax
 import jax.numpy as jnp
 from jax import lax
+from jax.experimental import pallas as pl
+from jax.experimental.pallas import tpu as pltpu
 from jax.sharding import PartitionSpec as P
 
 
@@ -33,11 +37,284 @@
     return lax.all_gather(quarter, "rep", axis=1, tiled=True)
 
 
+MESH = pl.DeviceIdType.MESH
+PAD = 128
+
+
+def dense_kernel(nz, tok_ref, logit_ref, ids_ref, wgu_ref, wd_ref, out_ref,
+                 rows, gate_w, up_w, down_w, hid, own, core_in, part, z_in, pair, x_in, cross, y_in,
+                 w_sem, ag_send, ag_recv, hid_send, hid_recv, core_send, core_recv,
+                 z_send, z_recv, x_send, x_recv, y_send, y_recv):
+    y = lax.axis_index("rep")
+    ep = lax.axis_index("ep")
+    z, x, c = ep // 4, (ep // 2) % 2, ep % 2
+    oy, ox, oc = 1 - y, 1 - x, 1 - c
+    q, width = tok_ref.shape
+    units = gate_w.shape[1]
+    cols = down_w.shape[1]
+    half = 2 * nz * q
+    full = 2 * half
+
+    def at(yy, zz, xx, cc):
+        return (yy, zz * 4 + xx * 2 + cc)
+
+    weights = [
+        pltpu.make_async_copy(wgu_ref.at[0, 0], gate_w, w_sem.at[0]),
+        pltpu.make_async_copy(wgu_ref.at[0, 1], up_w, w_sem.at[1]),
+        pltpu.make_async_copy(wd_ref.at[0], down_w, w_sem.at[2]),
+    ]
+    for w in weights:
+        w.start()
+
+    barrier = pltpu.get_barrier_semaphore()
+    peers = [at(oy, z, x, c), at(y, z, ox, c), at(y, z, x, oc)]
+    peers += [at(y, (z + d) % nz, x, c) for d in range(1, nz)]
+    for p in peers:
+        pl.semaphore_signal(barrier, inc=1, device_id=p, device_id_type=MESH)
+
+    scaled = jnp.exp(logit_ref[...])
+    soft = scaled / jnp.sum(scaled, axis=1, keepdims=True)
+    lane = lax.broadcasted_iota(jnp.int32, (q, PAD), 1)
+    n_ep = 4 * nz
+    expert, piece = lane % n_ep, lane // n_ep
+    ids = ids_ref[...]
+    comb = jnp.zeros((q, PAD), jnp.float32)
+    for k in range(ids.shape[1]):
+        comb = comb + jnp.where(ids[:, k:k + 1] == expert, soft[:, k:k + 1], 0.0)
+    hi = comb.astype(jnp.bfloat16).astype(jnp.float32)
+    rest = comb - hi
+    mid = rest.astype(jnp.bfloat16).astype(jnp.float32)
+    low = rest - mid
+    coded = jnp.where(piece == 0, hi, jnp.where(piece == 1, mid, jnp.where(piece == 2, low, 0.0)))
+    rows[x, c, z, y, :, :width] = tok_ref[...]
+    rows[x, c, z, y, :, width:] = coded.astype(jnp.bfloat16)
+    pl.semaphore_wait(barrier, len(peers))
+
+    sent = []
+
+    def flat(s):
+        return ((s[0] * 2 + s[1]) * nz + s[2]) * 2 + s[3]
+
+    def ag_copy(kind, s, dev):
+        return pltpu.make_async_remote_copy(
+            src_ref=rows.at[s[0], s[1], s[2], s[3]], dst_ref=rows.at[s[0], s[1], s[2], s[3]],
+            send_sem=ag_send.at[kind, flat(s)], recv_sem=ag_recv.at[flat(s)],
+            device_id=dev, device_id_type=MESH)
+
+    def send(kind, s, dev, cond=None):
+        def go():
+            ag_copy(kind, s, dev).start()
+        if cond is None:
+            go()
+        else:
+            pl.when(cond)(go)
+        sent.append((kind, s, dev, cond))
+
+    def arrive(s):
+        ag_copy(0, s, peers[0]).wait_recv()
+
+    up, down = at(y, jnp.minimum(z + 1, nz - 1), x, c), at(y, jnp.maximum(z - 1, 0), x, c)
+    mine = (x, c, z, y)
+    send(0, mine, peers[0])
+    send(1, mine, up, z < nz - 1)
+    send(2, mine, down, z > 0)
+    send(3, mine, peers[1])
+    send(4, mine, peers[2])
+    other = (x, c, z, oy)
+    arrive(other)
+    send(1, other, up, z < nz - 1)
+    send(2, other, down, z > 0)
+    send(3, other, peers[1])
+    send(4, other, peers[2])
+    for d in range(1, nz):
+        for rr in (y, oy):
+            below = (x, c, jnp.maximum(z - d, 0), rr)
+            above = (x, c, jnp.minimum(z + d, nz - 1), rr)
+            has_below, has_above = z >= d, z + d <= nz - 1
+
+            @pl.when(has_below)
+            def _():
+                arrive(below)
+            send(1, below, up, jnp.logical_and(has_below, z < nz - 1))
+            send(3, below, peers[1], has_below)
+            send(4, below, peers[2], has_below)
+
+            @pl.when(has_above)
+            def _():
+                arrive(above)
+            send(2, above, down, jnp.logical_and(has_above, z > 0))
+            send(3, above, peers[1], has_above)
+            send(4, above, peers[2], has_above)
+
+    def hid_copy(g):
+        return pltpu.make_async_remote_copy(
+            src_ref=hid.at[g, y], dst_ref=hid.at[g, y],
+            send_sem=hid_send.at[g], recv_sem=hid_recv.at[g],
+            device_id=peers[0], device_id_type=MESH)
+
+    def hidden_of(g, xx):
+        def tile(i, carry):
+            at_cols = pl.ds(pl.multiple_of(i * TILE, TILE), TILE)
+            block = rows[xx].reshape(full, width + PAD)[:, :width]
+            gate = jnp.dot(block, gate_w[:, at_cols], preferred_element_type=jnp.float32)
+            upper = jnp.dot(block, up_w[:, at_cols], preferred_element_type=jnp.float32)
+            hid[g, y, :, at_cols] = (jax.nn.silu(gate) * upper).astype(jnp.bfloat16)
+            return carry
+        lax.fori_loop(0, units // TILE, tile, 0)
+        hid_copy(g).start()
+
+    def core_copy(g):
+        return pltpu.make_async_remote_copy(
+            src_ref=own.at[g, oc], dst_ref=core_in.at[g],
+            send_sem=core_send.at[g], recv_sem=core_recv.at[g],
+            device_id=peers[2], device_id_type=MESH)
+
+    def z_copy(g, d):
+        to = (z + d) % nz
+        return pltpu.make_async_remote_copy(
+            src_ref=part.at[g, to], dst_ref=z_in.at[g, d - 1],
+            send_sem=z_send.at[g, d - 1], recv_sem=z_recv.at[g, d - 1],
+            device_id=at(y, to, x, c), device_id_type=MESH)
+
+    def outputs_of(g, xx):
+        hid_copy(g).wait_recv()
+        picked = lax.broadcasted_iota(jnp.int32, (full, PAD), 1)
+        keep = jnp.logical_and(picked % n_ep == ep, picked < 3 * n_ep)
+        codes = rows[xx].reshape(full, width + PAD)[:, width:].astype(jnp.float32)
+        weight = jnp.sum(jnp.where(keep, codes, 0.0), axis=1, keepdims=True)
+
+        def tile(i, carry):
+            at_cols = pl.ds(pl.multiple_of(i * TILE, TILE), TILE)
+            total = jnp.dot(hid[g, 0], down_w[:units, at_cols], preferred_element_type=jnp.float32)
+            total += jnp.dot(hid[g, 1], down_w[units:, at_cols], preferred_element_type=jnp.float32)
+            value = total.astype(jnp.bfloat16).astype(jnp.float32) * weight
+            own[g, :, :, at_cols] = value.astype(jnp.bfloat16).reshape(2, half, TILE)
+            return carry
+        lax.fori_loop(0, cols // TILE, tile, 0)
+        core_copy(g).start()
+
+    def over_z(g):
+        core_copy(g).wait_recv()
+        for d in list(range(1, nz)) + [0]:
+            to = (z + d) % nz
+            at_rows = pl.ds(pl.multiple_of(to * 2 * q, 2 * q), 2 * q)
+            total = own[g, c, at_rows, :].astype(jnp.float32) + core_in[g, at_rows, :].astype(jnp.float32)
+            part[g, to] = total.astype(jnp.bfloat16)
+            if d:
+                z_copy(g, d).start()
+
+    def z_total(g):
+        total = part[g, z].astype(jnp.float32)
+        for d in range(1, nz):
+            z_copy(g, d).wait_recv()
+            total = total + z_in[g, d - 1].astype(jnp.float32)
+        return total
+
+    for zz in range(nz):
+        for rr in range(2):
+            arrive((x, oc, zz, rr))
+    for w in weights[:2]:
+        w.wait()
+    hidden_of(0, x)
+    for zz in range(nz):
+        for rr in range(2):
+            s = (ox, c, zz, rr)
+            arrive(s)
+            send(4, s, peers[2])
+    for zz in range(nz):
+        for rr in range(2):
+            arrive((ox, oc, zz, rr))
+    hidden_of(1, ox)
+    weights[2].wait()
+    outputs_of(0, x)
+    over_z(0)
+    outputs_of(1, ox)
+    over_z(1)
+
+    x_copy = pltpu.make_async_remote_copy(
+        src_ref=pair, dst_ref=x_in, send_sem=x_send, recv_sem=x_recv,
+        device_id=peers[1], device_id_type=MESH)
+    y_copy = pltpu.make_async_remote_copy(
+        src_ref=cross.at[oy], dst_ref=y_in, send_sem=y_send, recv_sem=y_recv,
+        device_id=peers[0], device_id_type=MESH)
+    near = z_total(0)
+    pair[...] = z_total(1).astype(jnp.bfloat16)
+    x_copy.start()
+    x_copy.wait_recv()
+    final = (near + x_in[...].astype(jnp.float32)).astype(jnp.bfloat16)
+    cross[...] = final.reshape(2, q, cols)
+    y_copy.start()
+    out_ref[:, pl.ds(pl.multiple_of(y * cols, cols), cols)] = cross[y]
+    y_copy.wait_recv()
+    out_ref[:, pl.ds(pl.multiple_of(oy * cols, cols), cols)] = y_in[...]
+
+    for kind, s, dev, cond in sent:
+        def done(kind=kind, s=s, dev=dev):
+            ag_copy(kind, s, dev).wait_send()
+        if cond is None:
+            done()
+        else:
+            pl.when(cond)(done)
+    for g in range(2):
+        hid_copy(g).wait_send()
+        core_copy(g).wait_send()
+        for d in range(1, nz):
+            z_copy(g, d).wait_send()
+    x_copy.wait_send()
+    y_copy.wait_send()
+
+
+TILE = 256
+
+
+def dense_body(tokens, logits, expert_ids, w_gate_up, w_down):
+    nz = lax.axis_size("ep") // 4
+    q, width = tokens.shape
+    units = w_gate_up.shape[3]
+    cols = w_down.shape[2]
+    half = 2 * nz * q
+    bf, sem = jnp.bfloat16, pltpu.SemaphoreType.DMA
+    vmem = pl.BlockSpec(memory_space=pltpu.VMEM)
+    hbm = pl.BlockSpec(memory_space=pl.ANY)
+    return pl.pallas_call(
+        functools.partial(dense_kernel, nz),
+        out_shape=jax.ShapeDtypeStruct((q, width), bf),
+        in_specs=[vmem, vmem, vmem, hbm, hbm],
+        out_specs=vmem,
+        scratch_shapes=[
+            pltpu.VMEM((2, 2, nz, 2, q, width + PAD), bf),
+            pltpu.VMEM((width, units), bf),
+            pltpu.VMEM((width, units), bf),
+            pltpu.VMEM((2 * units, cols), bf),
+            pltpu.VMEM((2, 2, 2 * half, units), bf),
+            pltpu.VMEM((2, 2, half, cols), bf),
+            pltpu.VMEM((2, half, cols), bf),
+            pltpu.VMEM((2, nz, 2 * q, cols), bf),
+            pltpu.VMEM((2, nz - 1, 2 * q, cols), bf),
+            pltpu.VMEM((2 * q, cols), bf),
+            pltpu.VMEM((2 * q, cols), bf),
+            pltpu.VMEM((2, q, cols), bf),
+            pltpu.VMEM((q, cols), bf),
+            sem((3,)),
+            sem((5, 8 * nz)), sem((8 * nz,)),
+            sem((2,)), sem((2,)),
+            sem((2,)), sem((2,)),
+            sem((2, nz - 1)), sem((2, nz - 1)),
+            sem, sem, sem, sem,
+        ],
+        compiler_params=pltpu.CompilerParams(
+            collective_id=0, has_side_effects=True, vmem_limit_bytes=48 * 1024 * 1024
+        ),
+    )(tokens, logits, expert_ids, w_gate_up, w_down)
+
+
 def body(tokens, logits, expert_ids, w_gate_up, w_down):
     expert_count = lax.axis_size("ep")
     queue_len, picks = expert_ids.shape
     features = tokens.shape[1]
     capacity = max(2, min(queue_len, 2 * queue_len * picks // expert_count))
+    if capacity == queue_len and lax.axis_size("rep") == 2 and expert_count % 8 == 0 and 3 * expert_count <= PAD:
+        return dense_body(tokens, logits, expert_ids, w_gate_up, w_down)
     slot_total = expert_count * capacity
     onehot = slot_plan(expert_ids, expert_count, capacity)
     scaled = jnp.exp(logits)

time: 175 us -> 62.1 us (0.35)
  waiting for transfers between devices: 83.7 us -> 0 us
  Pallas kernels: 0 us -> 57 us
  blocking collectives: 48.1 us -> 0 us
  matrix products: 16 us -> 0 us
  between operations: 13.5 us -> 0.01 us
  starting transfers between devices: 5.71 us -> 0 us
    all_gather x2 -> x0, waiting for transfers between devices: 60.9 us -> none  [the longest x1 33.6 us: body(): portion = lax.all_gather(slot_rows, 'rep', axis=0, tiled=True)]
    pallas_call x0 -> x1, Pallas kernels: none -> 57 us  [dense_body(): pl.pallas_call(functools.partial(dense_kernel, nz), out_shape=jax.ShapeDt...]
    all_to_all x2 -> x0, blocking collectives: 48.1 us -> none  [the longest x1 32 us: to_owners(): lax.all_to_all(outgoing, 'ep', split_axis=0, concat_axis=0, tiled=True)]
    all_to_all x1 -> x0, waiting for transfers between devices: 22.7 us -> none  [to_sources(): lax.all_to_all(results, 'ep', split_axis=0, concat_axis=0, tiled=True)]
    dot_general x5 -> x0, matrix products: 16 us -> none  [the longest x1 4.68 us: body(): upper = jnp.dot(portion, up_weight, preferred_element_type=jnp.float32)]
    all_to_all x1 -> x0, starting transfers between devices: 5.67 us -> none  [to_sources(): lax.all_to_all(results, 'ep', split_axis=0, concat_axis=0, tiled=True)]
    unnamed x7, local copies, waits for them, and re-layouts: 0.92 us -> 4.87 us
    reshape x1 -> x0, local copies, waits for them, and re-layouts: 2.64 us -> none  [body(): returned = to_sources(own_rows.reshape(expert_count, capacity, features))]
  transfers between devices with their start and end apart: 3 -> 0, of which waited for: 3 -> 0; matrix products, arithmetic and copies ran while one was open for 0% -> 0% of each run, Pallas kernels for 0% -> 0%
where the time goes in v1:
time: 62.1 us; the launch traced here: 61.9 us
  Pallas kernels  57 us (92%)
  local copies, waits for them, and re-layouts  4.87 us (8%)
    pallas_call x1, Pallas kernels, dense_body(): pl.pallas_call(functools.partial(dense_kernel, nz), out_shape=jax.ShapeDt...  57 us
    unnamed x7, local copies, waits for them, and re-layouts  4.87 us

profile of v1, /device:TPU:0, one launch (start us, length us, event | category | flops | bytes accessed | tf_op | source)
XLA Modules:
  0.0 61.9 jit_solution(11950624365643394536)
XLA Ops:
  0.0 0.8 %copy.6.logit_ref = f32[16,8]{1,0:T(8,128)S(1)} copy(f32[16,8]{0,1:T(8,128)} %param.6) | data formatting | bytes 1024 | tf_op args[1]
  0.8 0.8 %copy.7.ids_ref = s32[16,8]{1,0:T(8,128)S(1)} copy(s32[16,8]{0,1:T(8,128)} %param.7) | data formatting | bytes 1024 | tf_op args[2]
  1.5 0.0 copy-start
  1.5 1.9 %copy-done = bf16[1,1536,1024]{2,1,0:T(8,128)(2,1)S(1)} copy-done((bf16[1,1536,1024]{2,1,0:T(8,128)(2,1)S(1)}, bf16[1,1536,1024]{2,1,0:T(8,128)(2,1)}, u32[]{:S(2)}) %copy-start) | copy-done | bytes 3145752
  3.4 0.0 copy-start.1
  3.4 0.8 %copy-done.1 = bf16[16,2048]{1,0:T(8,128)(2,1)S(1)} copy-done((bf16[16,2048]{1,0:T(8,128)(2,1)S(1)}, bf16[16,2048]{1,0:T(8,128)(2,1)}, u32[]{:S(2)}) %copy-start.1) | copy-done | bytes 65560
  4.2 57.0 %shard_map.55 = bf16[16,2048]{1,0:T(8,128)(2,1)S(1)} custom-call(bf16[16,2048]{1,0:T(8,128)(2,1)S(1)} %copy-done.1, f32[16,8]{1,0:T(8,128)S(1)} %copy.6.logit_ref, s32[16,8]{1,0:T(8,128)S(1)} %copy.7.ids_ref, bf16[1,2,2048,768]{3,2,1,0:T(8,128)(2,1)} %wgu_ref.1, bf16[1,1536,1024]{2,1,0:T(8,128)(2,1)S(1)} %copy-done), custom_call_target="tpu_custom_call" | custom-call | tf_op jit(solution)/shard_map/pallas_call | solution.py:279
  61.2 0.6 %copy.9 = bf16[16,2048]{1,0:T(8,128)(2,1)} copy(bf16[16,2048]{1,0:T(8,128)(2,1)S(1)} %shard_map.55) | data formatting | bytes 131072
Async XLA Ops:
  1.5 1.9 %copy-start = (bf16[1,1536,1024]{2,1,0:T(8,128)(2,1)S(1)}, bf16[1,1536,1024]{2,1,0:T(8,128)(2,1)}, u32[]{:S(2)}) copy-start(bf16[1,1536,1024]{2,1,0:T(8,128)(2,1)} %wd_ref.1) | copy-start | bytes 9437188
  3.4 0.8 %copy-start.1 = (bf16[16,2048]{1,0:T(8,128)(2,1)S(1)}, bf16[16,2048]{1,0:T(8,128)(2,1)}, u32[]{:S(2)}) copy-start(bf16[16,2048]{1,0:T(8,128)(2,1)} %tok_ref.1) | copy-start | bytes 196612

commit v2 on v0

--- a/solution.py
+++ b/solution.py
@@ -1,6 +1,10 @@
+import functools
+
 import jax
 import jax.numpy as jnp
 from jax import lax
+from jax.experimental import pallas as pl
+from jax.experimental.pallas import tpu as pltpu
 from jax.sharding import PartitionSpec as P
 
 
@@ -33,11 +37,293 @@
     return lax.all_gather(quarter, "rep", axis=1, tiled=True)
 
 
+MESH = pl.DeviceIdType.MESH
+PAD = 128
+
+
+def dense_kernel(nz, tok_ref, logit_ref, ids_ref, wgu_ref, wd_ref, out_ref,
+                 rows, logit_v, ids_v, gate_w, up_w, down_w, hid, own, core_in, pair, keep, x_in,
+                 part, z_in, cross, y_in,
+                 w_sem, ag_send, ag_recv, hid_send, hid_recv, core_send, core_recv,
+                 x_send, x_recv, z_send, z_recv, y_send, y_recv):
+    y = lax.axis_index("rep")
+    ep = lax.axis_index("ep")
+    z, x, c = ep // 4, (ep // 2) % 2, ep % 2
+    oy, ox, oc = 1 - y, 1 - x, 1 - c
+    q, width = tok_ref.shape
+    units = gate_w.shape[1]
+    cols = down_w.shape[1]
+    chunk = 8 * q
+    n_ep = 4 * nz
+
+    def at(yy, zz, xx, cc):
+        return (yy, zz * 4 + xx * 2 + cc)
+
+    small = [
+        pltpu.make_async_copy(logit_ref, logit_v, w_sem.at[3]),
+        pltpu.make_async_copy(ids_ref, ids_v, w_sem.at[4]),
+        pltpu.make_async_copy(tok_ref, rows.at[z, x, c, y, :, pl.ds(0, width)], w_sem.at[5]),
+    ]
+    weights = [
+        pltpu.make_async_copy(wgu_ref.at[0, 0], gate_w, w_sem.at[0]),
+        pltpu.make_async_copy(wgu_ref.at[0, 1], up_w, w_sem.at[1]),
+        pltpu.make_async_copy(wd_ref.at[0], down_w, w_sem.at[2]),
+    ]
+    for w in small + weights:
+        w.start()
+
+    barrier = pltpu.get_barrier_semaphore()
+    peers = [at(oy, z, x, c), at(y, z, ox, c), at(y, z, x, oc)]
+    peers += [at(y, (z + d) % nz, x, c) for d in range(1, nz)]
+    for p in peers:
+        pl.semaphore_signal(barrier, inc=1, device_id=p, device_id_type=MESH)
+
+    for w in small:
+        w.wait()
+    scaled = jnp.exp(logit_v[...])
+    soft = scaled / jnp.sum(scaled, axis=0, keepdims=True)
+    line = lax.broadcasted_iota(jnp.int32, (PAD, q), 0)
+    expert, piece = line % n_ep, line // n_ep
+    ids = ids_v[...]
+    comb = jnp.zeros((PAD, q), jnp.float32)
+    for k in range(ids.shape[0]):
+        comb = comb + jnp.where(ids[k:k + 1, :] == expert, soft[k:k + 1, :], 0.0)
+    hi = comb.astype(jnp.bfloat16).astype(jnp.float32)
+    rest = comb - hi
+    mid = rest.astype(jnp.bfloat16).astype(jnp.float32)
+    low = rest - mid
+    coded = jnp.where(piece == 0, hi, jnp.where(piece == 1, mid, jnp.where(piece == 2, low, 0.0)))
+    rows[z, x, c, y, :, width:] = coded.T.astype(jnp.bfloat16)
+    pl.semaphore_wait(barrier, len(peers))
+
+    sent = []
+
+    def ag_copy(kind, s, dev):
+        flat = ((s[0] * 2 + s[1]) * 2 + s[2]) * 2 + s[3]
+        return pltpu.make_async_remote_copy(
+            src_ref=rows.at[s[0], s[1], s[2], s[3]], dst_ref=rows.at[s[0], s[1], s[2], s[3]],
+            send_sem=ag_send.at[kind, flat], recv_sem=ag_recv.at[flat],
+            device_id=dev, device_id_type=MESH)
+
+    def send(kind, s, dev, cond=None):
+        def go():
+            ag_copy(kind, s, dev).start()
+        if cond is None:
+            go()
+        else:
+            pl.when(cond)(go)
+        sent.append((kind, s, dev, cond))
+
+    def arrive(s):
+        ag_copy(0, s, peers[0]).wait_recv()
+
+    near = jnp.minimum(z, nz - 1 - z)
+    rising = z < nz - 1 - z
+    order = [z]
+    for k in range(1, nz):
+        d = jnp.where(k <= 2 * near, (k + 1) // 2, k - near)
+        sign = jnp.where(k <= 2 * near, -1 if k % 2 else 1, jnp.where(rising, 1, -1))
+        order.append(z + sign * d)
+    up, down = at(y, jnp.minimum(z + 1, nz - 1), x, c), at(y, jnp.maximum(z - 1, 0), x, c)
+
+    def spread(s, go_up, go_down):
+        send(1, s, up, go_up)
+        send(2, s, down, go_down)
+        send(3, s, peers[1])
+        send(4, s, peers[2])
+
+    def along_z(k):
+        for rr in (y, oy):
+            s = (order[k], x, c, rr)
+            arrive(s)
+            spread(s, jnp.logical_and(order[k] < z, z < nz - 1), jnp.logical_and(order[k] > z, z > 0))
+
+    def along_x(k):
+        for rr in (y, oy):
+            s = (order[k], ox, c, rr)
+            arrive(s)
+            send(4, s, peers[2])
+
+    def hid_copy(k):
+        return pltpu.make_async_remote_copy(
+            src_ref=hid.at[k, y], dst_ref=hid.at[k, y],
+            send_sem=hid_send.at[k], recv_sem=hid_recv.at[k],
+            device_id=peers[0], device_id_type=MESH)
+
+    def hidden_of(k):
+        for xx in (x, ox):
+            for rr in (y, oy):
+                arrive((order[k], xx, oc, rr))
+
+        def tile(i, carry):
+            at_cols = pl.ds(pl.multiple_of(i * TILE, TILE), TILE)
+            block = rows[order[k]].reshape(chunk, width + PAD)[:, :width]
+            gate = jnp.dot(block, gate_w[:, at_cols], preferred_element_type=jnp.float32)
+            upper = jnp.dot(block, up_w[:, at_cols], preferred_element_type=jnp.float32)
+            hid[k, y, :, at_cols] = (jax.nn.silu(gate) * upper).astype(jnp.bfloat16)
+            return carry
+        lax.fori_loop(0, units // TILE, tile, 0)
+        hid_copy(k).start()
+
+    def core_copy(k):
+        return pltpu.make_async_remote_copy(
+            src_ref=own.at[k, oc], dst_ref=core_in.at[k],
+            send_sem=core_send.at[k], recv_sem=core_recv.at[k],
+            device_id=peers[2], device_id_type=MESH)
+
+    def x_copy(k):
+        return pltpu.make_async_remote_copy(
+            src_ref=pair.at[k], dst_ref=x_in.at[k],
+            send_sem=x_send.at[k], recv_sem=x_recv.at[k],
+            device_id=peers[1], device_id_type=MESH)
+
+    def z_copy(k, slot):
+        return pltpu.make_async_remote_copy(
+            src_ref=part.at[k], dst_ref=z_in.at[slot],
+            send_sem=z_send.at[k], recv_sem=z_recv.at[slot],
+            device_id=at(y, order[k], x, c), device_id_type=MESH)
+
+    def outputs_of(k):
+        picked = lax.broadcasted_iota(jnp.int32, (chunk, PAD), 1)
+        take = jnp.logical_and(picked % n_ep == ep, picked < 3 * n_ep)
+        codes = rows[order[k]].reshape(chunk, width + PAD)[:, width:].astype(jnp.float32)
+        weight = jnp.sum(jnp.where(take, codes, 0.0), axis=1, keepdims=True)
+        hid_copy(k).wait_recv()
+
+        def tile(i, carry):
+            at_cols = pl.ds(pl.multiple_of(i * TILE, TILE), TILE)
+            total = jnp.dot(hid[k, 0], down_w[:units, at_cols], preferred_element_type=jnp.float32)
+            total += jnp.dot(hid[k, 1], down_w[units:, at_cols], preferred_element_type=jnp.float32)
+            value = (total.astype(jnp.bfloat16).astype(jnp.float32) * weight).astype(jnp.bfloat16)
+            for a in range(2):
+                for b in range(2):
+                    own[k, b, a, :, at_cols] = value[(a * 2 + b) * 2 * q:(a * 2 + b + 1) * 2 * q]
+            return carry
+        lax.fori_loop(0, cols // TILE, tile, 0)
+        core_copy(k).start()
+
+    def over_core(k):
+        core_copy(k).wait_recv()
+        far = own[k, c, ox].astype(jnp.float32) + core_in[k, ox].astype(jnp.float32)
+        pair[k] = far.astype(jnp.bfloat16)
+        x_copy(k).start()
+        keep[k] = own[k, c, x].astype(jnp.float32) + core_in[k, x].astype(jnp.float32)
+
+    def over_x(k):
+        x_copy(k).wait_recv()
+        total = keep[k] + x_in[k].astype(jnp.float32)
+        if k:
+            part[k] = total.astype(jnp.bfloat16)
+            z_copy(k, z).start()
+        else:
+            keep[k] = total
+
+    mine, other = (z, x, c, y), (z, x, c, oy)
+    send(0, mine, peers[0])
+    spread(mine, z < nz - 1, z > 0)
+    arrive(other)
+    spread(other, z < nz - 1, z > 0)
+    for k in range(nz):
+        if k + 1 < nz:
+            along_z(k + 1)
+        along_x(k)
+        if k == 0:
+            for w in weights[:2]:
+                w.wait()
+        hidden_of(k)
+    weights[2].wait()
+    for k in range(nz + 2):
+        if k < nz:
+            outputs_of(k)
+        if 0 <= k - 2:
+            over_x(k - 2)
+        if 0 <= k - 1 < nz:
+            over_core(k - 1)
+
+    total = keep[0]
+    for k in range(1, nz):
+        z_copy(k, order[k]).wait_recv()
+        total = total + z_in[order[k]].astype(jnp.float32)
+    cross[...] = total.astype(jnp.bfloat16).reshape(2, q, cols)
+    y_copy = pltpu.make_async_remote_copy(
+        src_ref=cross.at[oy], dst_ref=y_in, send_sem=y_send, recv_sem=y_recv,
+        device_id=peers[0], device_id_type=MESH)
+    y_copy.start()
+    out_ref[:, pl.ds(pl.multiple_of(y * cols, cols), cols)] = cross[y]
+
+    for kind, s, dev, cond in sent:
+        def done(kind=kind, s=s, dev=dev):
+            ag_copy(kind, s, dev).wait_send()
+        if cond is None:
+            done()
+        else:
+            pl.when(cond)(done)
+    for k in range(nz):
+        hid_copy(k).wait_send()
+        core_copy(k).wait_send()
+        x_copy(k).wait_send()
+        if k:
+            z_copy(k, z).wait_send()
+    y_copy.wait_send()
+    y_copy.wait_recv()
+    out_ref[:, pl.ds(pl.multiple_of(oy * cols, cols), cols)] = y_in[...]
+
+
+TILE = 256
+
+
+def dense_body(tokens, logits, expert_ids, w_gate_up, w_down):
+    nz = lax.axis_size("ep") // 4
+    q, width = tokens.shape
+    picks = logits.shape[1]
+    units = w_gate_up.shape[3]
+    cols = w_down.shape[2]
+    bf, sem = jnp.bfloat16, pltpu.SemaphoreType.DMA
+    vmem = pl.BlockSpec(memory_space=pltpu.VMEM)
+    hbm = pl.BlockSpec(memory_space=pl.ANY)
+    return pl.pallas_call(
+        functools.partial(dense_kernel, nz),
+        out_shape=jax.ShapeDtypeStruct((q, width), bf),
+        in_specs=[hbm] * 5,
+        out_specs=vmem,
+        scratch_shapes=[
+            pltpu.VMEM((nz, 2, 2, 2, q, width + PAD), bf),
+            pltpu.VMEM((picks, q), jnp.float32),
+            pltpu.VMEM((picks, q), jnp.int32),
+            pltpu.VMEM((width, units), bf),
+            pltpu.VMEM((width, units), bf),
+            pltpu.VMEM((2 * units, cols), bf),
+            pltpu.VMEM((nz, 2, 8 * q, units), bf),
+            pltpu.VMEM((nz, 2, 2, 2 * q, cols), bf),
+            pltpu.VMEM((nz, 2, 2 * q, cols), bf),
+            pltpu.VMEM((nz, 2 * q, cols), bf),
+            pltpu.VMEM((nz, 2 * q, cols), jnp.float32),
+            pltpu.VMEM((nz, 2 * q, cols), bf),
+            pltpu.VMEM((nz, 2 * q, cols), bf),
+            pltpu.VMEM((nz, 2 * q, cols), bf),
+            pltpu.VMEM((2, q, cols), bf),
+            pltpu.VMEM((q, cols), bf),
+            sem((6,)),
+            sem((5, 8 * nz)), sem((8 * nz,)),
+            sem((nz,)), sem((nz,)),
+            sem((nz,)), sem((nz,)),
+            sem((nz,)), sem((nz,)),
+            sem((nz,)), sem((nz,)),
+            sem, sem,
+        ],
+        compiler_params=pltpu.CompilerParams(
+            collective_id=0, has_side_effects=True, vmem_limit_bytes=60 * 1024 * 1024
+        ),
+    )(tokens, logits.T, expert_ids.T, w_gate_up, w_down)
+
+
 def body(tokens, logits, expert_ids, w_gate_up, w_down):
     expert_count = lax.axis_size("ep")
     queue_len, picks = expert_ids.shape
     features = tokens.shape[1]
     capacity = max(2, min(queue_len, 2 * queue_len * picks // expert_count))
+    if capacity == queue_len and lax.axis_size("rep") == 2 and expert_count % 8 == 0 and 3 * expert_count <= PAD:
+        return dense_body(tokens, logits, expert_ids, w_gate_up, w_down)
     slot_total = expert_count * capacity
     onehot = slot_plan(expert_ids, expert_count, capacity)
     scaled = jnp.exp(logits)

time: 175 us -> 55.5 us (0.32)
  waiting for transfers between devices: 83.7 us -> 0 us
  Pallas kernels: 0 us -> 53.8 us
  blocking collectives: 48.1 us -> 0 us
  matrix products: 16 us -> 0 us
  between operations: 13.5 us -> 0.01 us
  starting transfers between devices: 5.71 us -> 0 us
  local copies, waits for them, and re-layouts: 5.91 us -> 1.47 us
    all_gather x2 -> x0, waiting for transfers between devices: 60.9 us -> none  [the longest x1 33.6 us: body(): portion = lax.all_gather(slot_rows, 'rep', axis=0, tiled=True)]
    pallas_call x0 -> x1, Pallas kernels: none -> 53.8 us  [dense_body(): pl.pallas_call(functools.partial(dense_kernel, nz), out_shape=jax.ShapeDt...]
    all_to_all x2 -> x0, blocking collectives: 48.1 us -> none  [the longest x1 32 us: to_owners(): lax.all_to_all(outgoing, 'ep', split_axis=0, concat_axis=0, tiled=True)]
    all_to_all x1 -> x0, waiting for transfers between devices: 22.7 us -> none  [to_sources(): lax.all_to_all(results, 'ep', split_axis=0, concat_axis=0, tiled=True)]
    dot_general x5 -> x0, matrix products: 16 us -> none  [the longest x1 4.68 us: body(): upper = jnp.dot(portion, up_weight, preferred_element_type=jnp.float32)]
    all_to_all x1 -> x0, starting transfers between devices: 5.67 us -> none  [to_sources(): lax.all_to_all(results, 'ep', split_axis=0, concat_axis=0, tiled=True)]
    reshape x1 -> x0, local copies, waits for them, and re-layouts: 2.64 us -> none  [body(): returned = to_sources(own_rows.reshape(expert_count, capacity, features))]
    all_to_all x1 -> x0, local copies, waits for them, and re-layouts: 2.11 us -> none  [body(): lax.all_to_all(partial_out, 'rep', split_axis=0, concat_axis=1, tiled=True)]
  transfers between devices with their start and end apart: 3 -> 0, of which waited for: 3 -> 0; matrix products, arithmetic and copies ran while one was open for 0% -> 0% of each run, Pallas kernels for 0% -> 0%
where the time goes in v2:
time: 55.5 us; the launch traced here: 55.3 us
  Pallas kernels  53.8 us (97%)
  local copies, waits for them, and re-layouts  1.47 us (3%)
    pallas_call x1, Pallas kernels, dense_body(): pl.pallas_call(functools.partial(dense_kernel, nz), out_shape=jax.ShapeDt...  53.8 us
    unnamed x1, local copies, waits for them, and re-layouts  1.47 us

profile of v2, /device:TPU:0, one launch (start us, length us, event | category | flops | bytes accessed | tf_op | source)
XLA Modules:
  0.0 55.3 jit_solution(2802928186017678010)
XLA Ops:
  0.0 53.8 %shard_map.55 = bf16[16,2048]{1,0:T(8,128)(2,1)} custom-call(bf16[16,2048]{1,0:T(8,128)(2,1)} %tok_ref.1, f32[8,16]{1,0:T(8,128)} %bitcast.2, s32[8,16]{1,0:T(8,128)} %bitcast.3, bf16[1,2,2048,768]{3,2,1,0:T(8,128)(2,1)} %wgu_ref.1, bf16[1,1536,1024]{2,1,0:T(8,128)(2,1)} %wd_ref.1), custom_call_target="tpu_custom_call" | custom-call | tf_op jit(solution)/shard_map/pallas_call | solution.py:284
  53.8 1.5 %copy.7 = bf16[16,2048]{1,0:T(8,128)(2,1)} copy(bf16[16,2048]{1,0:T(8,128)(2,1)} %shard_map.55) | data formatting | bytes 131072

commit v3 on v2

--- a/solution.py
+++ b/solution.py
@@ -230,15 +230,28 @@
         if k == 0:
             for w in weights[:2]:
                 w.wait()
+        if k == nz - 1:
+            if nz > 2:
+                outputs_of(nz - 3)
+            for j in range(max(nz - 3, 0)):
+                over_core(j)
         hidden_of(k)
-    weights[2].wait()
-    for k in range(nz + 2):
+        if k == nz - 2:
+            weights[2].wait()
+            for j in range(max(nz - 3, 0)):
+                outputs_of(j)
+    if nz < 2:
+        weights[2].wait()
+    for k in range(max(nz - 4, 0)):
+        over_x(k)
+    for k in range(max(nz - 3, 0), nz + 1):
+        if k > max(nz - 3, 0) or nz < 3:
+            if k < nz:
+                outputs_of(k)
+        if k > 0:
+            over_x(k - 1)
         if k < nz:
-            outputs_of(k)
-        if 0 <= k - 2:
-            over_x(k - 2)
-        if 0 <= k - 1 < nz:
-            over_core(k - 1)
+            over_core(k)
 
     total = keep[0]
     for k in range(1, nz):

time: 55.5 us -> 52.8 us (0.951)
  Pallas kernels: 53.8 us -> 51.1 us
    pallas_call x1, Pallas kernels: 53.8 us -> 51.1 us  [dense_body(): pl.pallas_call(functools.partial(dense_kernel, nz), out_shape=jax.ShapeDt...]
where the time goes in v3:
time: 52.8 us; the launch traced here: 52.6 us
  Pallas kernels  51.1 us (97%)
  local copies, waits for them, and re-layouts  1.47 us (3%)
    pallas_call x1, Pallas kernels, dense_body(): pl.pallas_call(functools.partial(dense_kernel, nz), out_shape=jax.ShapeDt...  51.1 us
    unnamed x1, local copies, waits for them, and re-layouts  1.47 us

profile of v3, /device:TPU:0, one launch (start us, length us, event | category | flops | bytes accessed | tf_op | source)
XLA Modules:
  0.0 52.6 jit_solution(3746697067826359428)
XLA Ops:
  0.0 51.1 %shard_map.55 = bf16[16,2048]{1,0:T(8,128)(2,1)} custom-call(bf16[16,2048]{1,0:T(8,128)(2,1)} %tok_ref.1, f32[8,16]{1,0:T(8,128)} %bitcast.2, s32[8,16]{1,0:T(8,128)} %bitcast.3, bf16[1,2,2048,768]{3,2,1,0:T(8,128)(2,1)} %wgu_ref.1, bf16[1,1536,1024]{2,1,0:T(8,128)(2,1)} %wd_ref.1), custom_call_target="tpu_custom_call" | custom-call | tf_op jit(solution)/shard_map/pallas_call | solution.py:297
  51.1 1.5 %copy.7 = bf16[16,2048]{1,0:T(8,128)(2,1)} copy(bf16[16,2048]{1,0:T(8,128)(2,1)} %shard_map.55) | data formatting | bytes 131072

commit v4 on v3

--- a/solution.py
+++ b/solution.py
@@ -144,10 +144,11 @@
             arrive(s)
             send(4, s, peers[2])
 
-    def hid_copy(k):
-        return pltpu.make_async_remote_copy(
-            src_ref=hid.at[k, y], dst_ref=hid.at[k, y],
-            send_sem=hid_send.at[k], recv_sem=hid_recv.at[k],
+    def hid_copy(k, i):
+        at_cols = pl.ds(pl.multiple_of(i * TILE, TILE), TILE)
+        return pltpu.make_async_remote_copy(
+            src_ref=hid.at[k, y, :, at_cols], dst_ref=hid.at[k, y, :, at_cols],
+            send_sem=hid_send.at[k, i], recv_sem=hid_recv.at[k, i],
             device_id=peers[0], device_id_type=MESH)
 
     def hidden_of(k):
@@ -161,9 +162,9 @@
             gate = jnp.dot(block, gate_w[:, at_cols], preferred_element_type=jnp.float32)
             upper = jnp.dot(block, up_w[:, at_cols], preferred_element_type=jnp.float32)
             hid[k, y, :, at_cols] = (jax.nn.silu(gate) * upper).astype(jnp.bfloat16)
+            hid_copy(k, i).start()
             return carry
         lax.fori_loop(0, units // TILE, tile, 0)
-        hid_copy(k).start()
 
     def core_copy(k):
         return pltpu.make_async_remote_copy(
@@ -188,7 +189,8 @@
         take = jnp.logical_and(picked % n_ep == ep, picked < 3 * n_ep)
         codes = rows[order[k]].reshape(chunk, width + PAD)[:, width:].astype(jnp.float32)
         weight = jnp.sum(jnp.where(take, codes, 0.0), axis=1, keepdims=True)
-        hid_copy(k).wait_recv()
+        for i in range(units // TILE):
+            hid_copy(k, i).wait_recv()
 
         def tile(i, carry):
             at_cols = pl.ds(pl.multiple_of(i * TILE, TILE), TILE)
@@ -272,7 +274,8 @@
         else:
             pl.when(cond)(done)
     for k in range(nz):
-        hid_copy(k).wait_send()
+        for i in range(units // TILE):
+            hid_copy(k, i).wait_send()
         core_copy(k).wait_send()
         x_copy(k).wait_send()
         if k:
@@ -318,7 +321,7 @@
             pltpu.VMEM((q, cols), bf),
             sem((6,)),
             sem((5, 8 * nz)), sem((8 * nz,)),
-            sem((nz,)), sem((nz,)),
+            sem((nz, units // TILE)), sem((nz, units // TILE)),
             sem((nz,)), sem((nz,)),
             sem((nz,)), sem((nz,)),
             sem((nz,)), sem((nz,)),

time: 52.8 us -> 52 us (0.985)
  Pallas kernels: 51.1 us -> 50.4 us
    pallas_call x1, Pallas kernels: 51.1 us -> 50.4 us  [dense_body(): pl.pallas_call(functools.partial(dense_kernel, nz), out_shape=jax.ShapeDt...]
where the time goes in v4:
time: 52 us; the launch traced here: 51.9 us
  Pallas kernels  50.4 us (97%)
  local copies, waits for them, and re-layouts  1.47 us (3%)
    pallas_call x1, Pallas kernels, dense_body(): pl.pallas_call(functools.partial(dense_kernel, nz), out_shape=jax.ShapeDt...  50.4 us
    unnamed x1, local copies, waits for them, and re-layouts  1.47 us

profile of v4, /device:TPU:0, one launch (start us, length us, event | category | flops | bytes accessed | tf_op | source)
XLA Modules:
  0.0 51.9 jit_solution(8768721402525451665)
XLA Ops:
  0.0 50.4 %shard_map.55 = bf16[16,2048]{1,0:T(8,128)(2,1)} custom-call(bf16[16,2048]{1,0:T(8,128)(2,1)} %tok_ref.1, f32[8,16]{1,0:T(8,128)} %bitcast.2, s32[8,16]{1,0:T(8,128)} %bitcast.3, bf16[1,2,2048,768]{3,2,1,0:T(8,128)(2,1)} %wgu_ref.1, bf16[1,1536,1024]{2,1,0:T(8,128)(2,1)} %wd_ref.1), custom_call_target="tpu_custom_call" | custom-call | tf_op jit(solution)/shard_map/pallas_call | solution.py:300
  50.4 1.5 %copy.7 = bf16[16,2048]{1,0:T(8,128)(2,1)} copy(bf16[16,2048]{1,0:T(8,128)(2,1)} %shard_map.55) | data formatting | bytes 131072
